TPU v7x, 32 devices: a whole 2x2x4 slice. The times are simulated.
32 devices in a mesh: row: 8 (over y, x, core), rep: 4 (over z).
Axes of the slice: x: 2, y: 2, z: 4, core: 2. Of those that a mesh axis runs over, the one named last changes fastest.
Arguments:
- features: bfloat16 [8192, 512], P(('row', 'rep')), may hold values from -6 to 6
- tiles: bfloat16 [64, 8, 128, 128], P(('row', 'rep')), may hold values from -0.1875 to 0.1875
- columns: int32 [64, 8], P(('row', 'rep')), may hold values from 0 to 63, as said below
- w_aggregate: bfloat16 [512, 512], replicated, may hold values from -0.25 to 0.25
- w_self: bfloat16 [512, 512], replicated, may hold values from -0.25 to 0.25
- w_middle: bfloat16 [512, 512], replicated, may hold values from -0.25 to 0.25
- w_output: bfloat16 [512, 512], replicated, may hold values from -0.25 to 0.25
- cotangent: bfloat16 [8192, 512], P(('row', 'rep')), may hold values from -6 to 6
Outputs:
- updated: bfloat16 [8192, 512], P(('row', 'rep'))
- grad_features: bfloat16 [8192, 512], P(('row', 'rep'))
- grad_output: float32 [512, 512], P('rep')
- grad_middle: float32 [512, 512], P('rep')
- grad_aggregate: float32 [512, 512], P('rep')
- grad_self: float32 [512, 512], P('rep')
Inputs may be any that keep to these rules, and one draw needn't show every extreme that they name: `columns`: row group g holds row blocks g * 8 to (g + 1) * 8 - 1, for g < 8. Every column block named by a row block of group g lies in group g - 1, g or g + 1, taken modulo 8; every row block names each of these three groups at least once. Column blocks may repeat within a row block.
All inputs are finite; a program needn't handle non-finite values.
Results may differ from a plain program's by a relative error of at most 0.015.
Values may be sent and summed in bfloat16 or wider, within the bound.
No kernel may reach another device: no remote copies, remote signals or barrier semaphores. Data moves between devices by JAX's collectives and lax.ppermute only.
A program may use at most 192 MiB of HBM per device.

v0:
```python
import math
import jax
import jax.numpy as jnp
from jax import lax
from jax.sharding import PartitionSpec as P


def from_behind(value, axis, steps):
    count = lax.axis_size(axis)
    pairs = [(source, (source + steps) % count) for source in range(count)]
    return lax.ppermute(value, axis, pairs)


def silu_slope(value):
    sig = jax.nn.sigmoid(value)
    return sig * (1.0 + value * (1.0 - sig))


def times_transposed(left_operand, weight):
    return lax.dot_general(
        left_operand, weight, (((1,), (1,)), ((), ())), preferred_element_type=jnp.float32
    )


def local(features, tiles, columns, w_aggregate, w_self, w_middle, w_output, cotangent):
    blocks_dev, width_k, tile_size, _ = tiles.shape
    width = features.shape[1]
    groups = lax.axis_size("row")
    replicas = lax.axis_size("rep")
    panel_blocks = replicas * blocks_dev
    panel_rows = panel_blocks * tile_size
    group_id = lax.axis_index("row")
    slot_of = (columns // panel_blocks - group_id + 1) % groups
    window_index = slot_of * panel_blocks + columns % panel_blocks
    own_panel = lax.all_gather(features, "rep", axis=0, tiled=True)
    prior_panel = from_behind(own_panel, "row", 1)
    next_panel = from_behind(own_panel, "row", -1)
    window = jnp.concatenate([prior_panel, own_panel, next_panel], 0).reshape(
        3 * panel_blocks, tile_size, width
    )
    picked = window[window_index]
    summed = jnp.einsum("bkij,bkjf->bif", tiles, picked, preferred_element_type=jnp.float32)
    aggregate = summed.reshape(blocks_dev * tile_size, width).astype(jnp.bfloat16)
    pre_first = jnp.dot(aggregate, w_aggregate, preferred_element_type=jnp.float32) + jnp.dot(
        features, w_self, preferred_element_type=jnp.float32
    )
    first = jax.nn.silu(pre_first).astype(jnp.bfloat16)
    pre_second = jnp.dot(first, w_middle, preferred_element_type=jnp.float32)
    second = jax.nn.silu(pre_second).astype(jnp.bfloat16)
    updated = (
        features.astype(jnp.float32) + jnp.dot(second, w_output, preferred_element_type=jnp.float32)
    ).astype(jnp.bfloat16)
    delta_second = (times_transposed(cotangent, w_output) * silu_slope(pre_second)).astype(
        jnp.bfloat16
    )
    delta_first = (times_transposed(delta_second, w_middle) * silu_slope(pre_first)).astype(
        jnp.bfloat16
    )
    delta_aggregate = times_transposed(delta_first, w_aggregate).astype(jnp.bfloat16)
    delta_blocks = delta_aggregate.reshape(blocks_dev, tile_size, width)
    messages = jnp.einsum("bkji,bjf->bkif", tiles, delta_blocks, preferred_element_type=jnp.float32)
    spread = jnp.zeros((3 * panel_blocks, tile_size, width), jnp.float32)
    spread = spread.at[window_index.reshape(-1)].add(messages.reshape(-1, tile_size, width))
    spread = spread.reshape(3 * panel_rows, width)
    prior_part = spread[:panel_rows]
    own_part = spread[panel_rows : 2 * panel_rows]
    next_part = spread[2 * panel_rows :]
    from_next = from_behind(prior_part.astype(jnp.bfloat16), "row", -1).astype(prior_part.dtype)
    from_prior = from_behind(next_part.astype(jnp.bfloat16), "row", 1).astype(next_part.dtype)
    returned = lax.psum_scatter(
        (own_part + from_next + from_prior).astype(jnp.bfloat16),
        "rep",
        scatter_dimension=0,
        tiled=True,
    ).astype(jnp.float32)
    grad_features = (
        cotangent.astype(jnp.float32) + times_transposed(delta_first, w_self) + returned
    ).astype(jnp.bfloat16)
    total_nodes = features.shape[0] * groups * replicas
    scale = 1.0 / math.sqrt(total_nodes)
    local_output = jnp.dot(second.T, cotangent, preferred_element_type=jnp.float32)
    local_middle = jnp.dot(first.T, delta_second, preferred_element_type=jnp.float32)
    local_aggregate = jnp.dot(aggregate.T, delta_first, preferred_element_type=jnp.float32)
    local_self = jnp.dot(features.T, delta_first, preferred_element_type=jnp.float32)
    shares = (
        lax.psum_scatter(
            local_output.astype(jnp.bfloat16), "rep", scatter_dimension=0, tiled=True
        ).astype(jnp.float32),
        lax.psum_scatter(
            local_middle.astype(jnp.bfloat16), "rep", scatter_dimension=0, tiled=True
        ).astype(jnp.float32),
        lax.psum_scatter(
            local_aggregate.astype(jnp.bfloat16), "rep", scatter_dimension=0, tiled=True
        ).astype(jnp.float32),
        lax.psum_scatter(
            local_self.astype(jnp.bfloat16), "rep", scatter_dimension=0, tiled=True
        ).astype(jnp.float32),
    )
    totals = (
        lax.psum(shares[0].astype(jnp.bfloat16), "row").astype(jnp.float32),
        lax.psum(shares[1].astype(jnp.bfloat16), "row").astype(jnp.float32),
        lax.psum(shares[2].astype(jnp.bfloat16), "row").astype(jnp.float32),
        lax.psum(shares[3].astype(jnp.bfloat16), "row").astype(jnp.float32),
    )
    return (
        updated,
        grad_features,
        totals[0] * scale,
        totals[1] * scale,
        totals[2] * scale,
        totals[3] * scale,
    )


def solution(mesh):
    placed = (
        P(("row", "rep"), None),
        P(("row", "rep"), None, None, None),
        P(("row", "rep"), None),
        P(),
        P(),
        P(),
        P(),
        P(("row", "rep"), None),
    )
    return jax.shard_map(
        local,
        mesh=mesh,
        in_specs=placed,
        out_specs=(
            P(("row", "rep"), None),
            P(("row", "rep"), None),
            P("rep", None),
            P("rep", None),
            P("rep", None),
            P("rep", None),
        ),
        check_vma=False,
    )
```

profile of v0, /device:TPU:0, one launch (start us, length us, event | category | flops | bytes accessed | tf_op | source)
XLA Modules:
  0.0 258.1 jit_solution(4128961649939991356)
XLA Ops:
  8.0 32.3 %all-gather.2.cloned.1.call-done = bf16[1024,512]{1,0:T(8,128)(2,1)} async-done(((bf16[256,512]{1,0:T(8,128)(2,1)}), bf16[1024,512]{1,0:T(8,128)(2,1)}) %all-gather.2.cloned.1.call-update) | async-done | bytes 1048592 | tf_op jit(solution)/shard_map/all_gather | solution.py:35
  42.4 22.6 %collective-permute-done.1 = bf16[1024,512]{1,0:T(8,128)(2,1)S(1)} collective-permute-done((bf16[1024,512]{1,0:T(8,128)(2,1)}, bf16[1024,512]{1,0:T(8,128)(2,1)S(1)}, u32[]{:S(2)}, u32[]{:S(2)}) %collective-permute-start.1) | collective-permute-done | bytes 1048608 | tf_op jit(solution)/shard_map/ppermute | solution.py:11
  65.1 1.8 collective-permute-done
  66.9 2.8 %pad_maximum_fusion = bf16[3072,512]{1,0:T(8,128)(2,1)} fusion(bf16[1024,512]{1,0:T(8,128)(2,1)S(1)} %collective-permute-done.1, bf16[1024,512]{1,0:T(8,128)(2,1)} %all-gather.2.cloned.1.call-done, bf16[1024,512]{1,0:T(8,128)(2,1)S(1)} %collective-permute-done), kind=kLoop, calls=%fused_computation.2 | loop fusion | flops 9437184 | bytes 6291456 | tf_op jit(solution)/shard_map/concatenate | solution.py:38
  69.7 2.6 gather_fusion
  76.7 1.4 fusion.6
  81.0 2.7 %fusion.15 = f32[2,512,8,128]{3,1,2,0:T(8,128)} fusion(bf16[2,128,512,1]{2,1,3,0:T(8,128)(2,1)S(1)} %bitcast.59, bf16[2,8,128,128]{3,2,1,0:T(8,128)(2,1)S(1)} %copy-done), kind=kOutput, calls=%fused_computation.49 | convolution fusion | flops 268435456 | bytes 4980736 | tf_op jit(solution)/shard_map/bkji,bjf->bkif/dot_general | solution.py:61
  83.6 5.4 %copy.15 = f32[16,128,512]{2,1,0:T(8,128)} copy(f32[16,128,512]{1,2,0:T(8,128)} %bitcast.54) | data formatting | bytes 8388608 | tf_op jit(solution)/shard_map/reshape | solution.py:63
  89.0 3.5 %broadcast_in_dim.8 = f32[24,128,512]{2,1,0:T(8,128)} broadcast(f32[]{:T(128)} %constant.53.clone.1), dimensions={} | broadcast | bytes 6291460 | tf_op jit(solution)/shard_map/broadcast_in_dim | solution.py:62
  92.5 9.6 %scatter_fusion = f32[24,128,512]{2,1,0:T(8,128)} fusion(f32[24,128,512]{2,1,0:T(8,128)} %broadcast_in_dim.8, s32[16]{0:T(128)S(1)} %fusion.10, f32[16,128,512]{2,1,0:T(8,128)} %copy.15), kind=kCustom, calls=%fused_computation.1 | custom fusion | flops 1048576 | bytes 12582976 | tf_op jit(solution)/shard_map/scatter-add | solution.py:63
  102.0 3.4 %convert.4 = bf16[24,128,512]{2,1,0:T(8,128)(2,1)S(1)} convert(f32[24,128,512]{2,1,0:T(8,128)} %scatter_fusion) | non-fusion elementwise | flops 1572864 | bytes 9437184 | tf_op jit(solution)/shard_map/convert.1
  105.4 1.6 fusion.13
  108.3 2.7 %collective-permute-start.2 = (bf16[1024,512]{1,0:T(8,128)(2,1)}, bf16[1024,512]{1,0:T(8,128)(2,1)}, u32[]{:S(2)}, u32[]{:S(2)}) collective-permute-start(bf16[1024,512]{1,0:T(8,128)(2,1)} %bitcast.12), channel_id=1, source_target_pairs={{0,28},{4,0},{8,4},{12,8},{16,12},{20,16},{24,20},{28,24},{1,29},{... | collective-permute-start | bytes 3145736 | tf_op jit(solution)/shard_map/ppermute | solution.py:11
  111.0 1.9 slice.22
  112.9 6.7 %reduce-scatter.12.cloned.1.call-done = bf16[128,512]{1,0:T(8,128)(2,1)} async-done(((bf16[512,512]{1,0:T(8,128)(2,1)}), bf16[128,512]{1,0:T(8,128)(2,1)}) %reduce-scatter.12.cloned.1.call-update) | async-done | bytes 131088 | tf_op jit(solution)/shard_map/reduce_scatter | solution.py:92
  119.5 22.2 %reduce-scatter.8.cloned.1.call-done = bf16[128,512]{1,0:T(8,128)(2,1)} async-done(((bf16[512,512]{1,0:T(8,128)(2,1)}), bf16[128,512]{1,0:T(8,128)(2,1)}) %reduce-scatter.8.cloned.1.call-update) | async-done | bytes 131088 | tf_op jit(solution)/shard_map/reduce_scatter | solution.py:86
  141.8 22.2 %reduce-scatter.14.cloned.1.call-done = bf16[128,512]{1,0:T(8,128)(2,1)} async-done(((bf16[512,512]{1,0:T(8,128)(2,1)}), bf16[128,512]{1,0:T(8,128)(2,1)}) %reduce-scatter.14.cloned.1.call-update) | async-done | bytes 131088 | tf_op jit(solution)/shard_map/reduce_scatter | solution.py:95
  164.1 3.2 %fusion.1 = bf16[1024,512]{1,0:T(8,128)(2,1)} fusion(f32[8,128,512]{2,1,0:T(8,128)S(1)} %slice.22, bf16[1024,512]{1,0:T(8,128)(2,1)} %collective-permute-done.3, bf16[1024,512]{1,0:T(8,128)(2,1)} %collective-permute-done.2), kind=kLoop, calls=%fused_computation.5 | loop fusion | flops 2621440 | bytes 5242880 | tf_op jit(solution)/shard_map/convert_element_type | solution.py:71
  167.4 2.3 fusion.4
  170.0 50.6 %all-reduce.3.cloned.1.call-done = (bf16[128,512]{1,0:T(8,128)(2,1)}, bf16[128,512]{1,0:T(8,128)(2,1)}, bf16[128,512]{1,0:T(8,128)(2,1)}, bf16[128,512]{1,0:T(8,128)(2,1)}) async-done(((bf16[128,512]{1,0:T(8,128)(2,1)}, bf16[128,512]{1,0:T(8,128)(2,1)}, bf16[128,512]{1,0:T(8,128)(2,1)}, bf16[128,512]{1,0:T(8,128)(2,1)}), (bf16[128,512]{1,0:T(8,128)(2,1)}, bf16[128,512]{1,0:T(8,128)(2,1)}, ...) | async-done | bytes 524304 | tf_op jit(solution)/shard_map/psum | solution.py:100
  220.6 1.8 convert_multiply_fusion.2
  222.4 1.8 convert_multiply_fusion
  224.2 25.3 %reduce-scatter.6.cloned.1.call-done = bf16[256,512]{1,0:T(8,128)(2,1)} async-done(((bf16[1024,512]{1,0:T(8,128)(2,1)}), bf16[256,512]{1,0:T(8,128)(2,1)}) %reduce-scatter.6.cloned.1.call-update) | async-done | bytes 262160 | tf_op jit(solution)/shard_map/reduce_scatter | solution.py:70
  249.6 1.7 add_convert_fusion
  (64 shorter events, 11.6 us)
Async XLA Ops:
  7.2 65.1 %copy-start = (bf16[2,8,128,128]{3,2,1,0:T(8,128)(2,1)S(1)}, bf16[2,8,128,128]{3,2,1,0:T(8,128)(2,1)}, u32[]{:S(2)}) copy-start(bf16[2,8,128,128]{3,2,1,0:T(8,128)(2,1)} %param.9) | copy-start | bytes 1572868
  7.2 33.1 %all-gather.2.cloned.1.call-start = ((), (), s32[]{:S(2)}) async-start(), calls=%async_computation.5 | async-start | bytes 1310720 | tf_op jit(solution)/shard_map/all_gather | solution.py:35
  7.9 104.9 %reduce-scatter.10.cloned.1.call-start = ((), (), s32[]{:S(2)}) async-start(), calls=%async_computation.8 | async-start | bytes 655360 | tf_op jit(solution)/shard_map/reduce_scatter | solution.py:89
  40.3 24.8 %collective-permute-start.1 = (bf16[1024,512]{1,0:T(8,128)(2,1)}, bf16[1024,512]{1,0:T(8,128)(2,1)S(1)}, u32[]{:S(2)}, u32[]{:S(2)}) collective-permute-start(bf16[1024,512]{1,0:T(8,128)(2,1)} %all-gather.2.cloned.1.call-done), channel_id=1, source_target_pairs={{0,28},{4,0},{8,4},{12,8},{16,12},{20,16},{24,20},{28,24},{1,29},{... | collective-permute-start | bytes 3145736 | tf_op jit(solution)/shard_map/ppermute | solution.py:11
  41.6 25.3 %collective-permute-start = (bf16[1024,512]{1,0:T(8,128)(2,1)}, bf16[1024,512]{1,0:T(8,128)(2,1)S(1)}, u32[]{:S(2)}, u32[]{:S(2)}) collective-permute-start(bf16[1024,512]{1,0:T(8,128)(2,1)} %all-gather.2.cloned.1.call-done), channel_id=1, source_target_pairs={{0,4},{4,8},{8,12},{12,16},{16,20},{20,24},{24,28},{28,0},{1,5},{5... | collective-permute-start | bytes 3145736 | tf_op jit(solution)/shard_map/ppermute | solution.py:11
  72.3 1.0 copy-start.4
  72.3 1.3 copy-start.1
  72.3 1.3 copy-start.2
  72.3 1.6 copy-start.8
  72.8 1.5 copy-start.6
  72.8 1.5 copy-start.10
  74.3 2.3 copy-start.11
  74.3 2.4 copy-start.9
  76.6 2.8 %copy-start.12 = (f32[256,512]{1,0:T(8,128)S(1)}, f32[256,512]{1,0:T(8,128)}, u32[]{:S(2)}) copy-start(f32[256,512]{1,0:T(8,128)} %copy-done.11) | copy-start | bytes 1572868
  76.6 43.0 %reduce-scatter.12.cloned.1.call-start = ((), (), s32[]{:S(2)}) async-start(), calls=%async_computation.9 | async-start | bytes 655360 | tf_op jit(solution)/shard_map/reduce_scatter | solution.py:92
  78.1 2.5 copy-start.5
  79.2 62.6 %reduce-scatter.8.cloned.1.call-start = ((), (), s32[]{:S(2)}) async-start(), calls=%async_computation.7 | async-start | bytes 655360 | tf_op jit(solution)/shard_map/reduce_scatter | solution.py:86
  80.6 83.5 %reduce-scatter.14.cloned.1.call-start = ((), (), s32[]{:S(2)}) async-start(), calls=%async_computation.10 | async-start | bytes 655360 | tf_op jit(solution)/shard_map/reduce_scatter | solution.py:95
  107.0 57.1 %collective-permute-start.3 = (bf16[1024,512]{1,0:T(8,128)(2,1)}, bf16[1024,512]{1,0:T(8,128)(2,1)}, u32[]{:S(2)}, u32[]{:S(2)}) collective-permute-start(bf16[1024,512]{1,0:T(8,128)(2,1)} %bitcast.13), channel_id=1, source_target_pairs={{0,4},{4,8},{8,12},{12,16},{16,20},{20,24},{24,28},{28,0},{1,5},{5... | collective-permute-start | bytes 3145736 | tf_op jit(solution)/shard_map/ppermute | solution.py:11
  108.2 112.4 %all-reduce.3.cloned.1.call-start = ((), (), s32[]{:S(2)}) async-start(), calls=%async_computation.11 | async-start | bytes 1048576 | tf_op jit(solution)/shard_map/psum | solution.py:100
  108.3 55.8 %collective-permute-start.2 = (bf16[1024,512]{1,0:T(8,128)(2,1)}, bf16[1024,512]{1,0:T(8,128)(2,1)}, u32[]{:S(2)}, u32[]{:S(2)}) collective-permute-start(bf16[1024,512]{1,0:T(8,128)(2,1)} %bitcast.12), channel_id=1, source_target_pairs={{0,28},{4,0},{8,4},{12,8},{16,12},{20,16},{24,20},{28,24},{1,29},{... | collective-permute-start | bytes 3145736 | tf_op jit(solution)/shard_map/ppermute | solution.py:11
  164.0 85.5 %reduce-scatter.6.cloned.1.call-start = ((), (), s32[]{:S(2)}) async-start(), calls=%async_computation.6 | async-start | bytes 1310720 | tf_op jit(solution)/shard_map/reduce_scatter | solution.py:70
  167.3 2.3 copy-start.3
  167.3 2.3 copy-start.7
  (1 other events, 0.7 us)
Sparse Core Ops, SparseCore 0:
  9.6 30.6 all-gather.1
  76.7 20.3 reduce-scatter.9
  99.4 20.0 reduce-scatter.11
  121.7 20.0 reduce-scatter.7
  143.9 20.0 reduce-scatter.13
  167.2 53.3 all-reduce.2
  222.9 26.6 reduce-scatter.5
where the time goes:
time: 259 us; the launch traced here: 258 us
  waiting for transfers between devices  185 us (71%)
  other arithmetic  25 us (10%)
  local copies, waits for them, and re-layouts  16.3 us (6%)
  between operations  14.4 us (6%)
  matrix products  13.4 us (5%)
  starting transfers between devices  4.32 us (2%)
    psum x1, waiting for transfers between devices, local(): lax.psum(shares[0].astype(jnp.bfloat16), 'row').astype(jnp.float32)  50.6 us
    all_gather x1, waiting for transfers between devices, local(): own_panel = lax.all_gather(features, 'rep', axis=0, tiled=True)  32.3 us
    reduce_scatter x1, waiting for transfers between devices, local(): lax.psum_scatter((own_part + from_next + from_prior).astype(jnp.bfloat16)...  25.3 us
    ppermute x4, waiting for transfers between devices, from_behind(): return lax.ppermute(value, axis, pairs)  24.5 us
    reduce_scatter x1, waiting for transfers between devices, local(): lax.psum_scatter(local_output.astype(jnp.bfloat16), 'rep', scatter_dimens...  22.2 us
    reduce_scatter x1, waiting for transfers between devices, local(): lax.psum_scatter(local_self.astype(jnp.bfloat16), 'rep', scatter_dimensio...  22.2 us
    scatter-add x1, other arithmetic, local(): spread.at[window_index.reshape(-1)]  9.55 us
    reduce_scatter x1, waiting for transfers between devices, local(): lax.psum_scatter(local_aggregate.astype(jnp.bfloat16), 'rep', scatter_dim...  6.68 us
  transfers between devices with their start and end apart: 11, of which 8 were waited for; matrix products, arithmetic and copies ran while one was open for 17% of the time, Pallas kernels for 0%

commit v1 on v0

--- a/solution.py
+++ b/solution.py
@@ -32,7 +32,12 @@
     group_id = lax.axis_index("row")
     slot_of = (columns // panel_blocks - group_id + 1) % groups
     window_index = slot_of * panel_blocks + columns % panel_blocks
-    own_panel = lax.all_gather(features, "rep", axis=0, tiled=True)
+    ring = [features]
+    for hop in range(3):
+        ring.append(lax.ppermute(ring[-1], "rep", [(dev, (dev + 1) % 4) for dev in range(4)]))
+    own_panel = jnp.roll(
+        jnp.concatenate(ring[::-1], axis=0), (lax.axis_index("rep") + 1) * ring[0].shape[0], axis=0
+    )
     prior_panel = from_behind(own_panel, "row", 1)
     next_panel = from_behind(own_panel, "row", -1)
     window = jnp.concatenate([prior_panel, own_panel, next_panel], 0).reshape(

time: 259 us -> 254 us (0.981)
  waiting for transfers between devices: 185 us -> 178 us
    all_gather x1 -> x0, waiting for transfers between devices: 32.3 us -> none  [local(): own_panel = lax.all_gather(features, 'rep', axis=0, tiled=True)]
    ppermute x0 -> x3, waiting for transfers between devices: none -> 26.2 us  [local(): lax.ppermute(ring[-1], 'rep', [(dev, (dev + 1) % 4) for dev in range(4)])]
    ppermute x0 -> x3, starting transfers between devices: none -> 3.11 us  [local(): lax.ppermute(ring[-1], 'rep', [(dev, (dev + 1) % 4) for dev in range(4)])]
  transfers between devices with their start and end apart: 11 -> 13, of which waited for: 8 -> 10; matrix products, arithmetic and copies ran while one was open for 17% -> 16% of each run, Pallas kernels for 0% -> 0%
where the time goes in v1:
time: 254 us; the launch traced here: 253 us
  waiting for transfers between devices  178 us (70%)
  other arithmetic  24.2 us (10%)
  local copies, waits for them, and re-layouts  17.7 us (7%)
  between operations  14.4 us (6%)
  matrix products  12.5 us (5%)
  starting transfers between devices  6.6 us (3%)
    psum x1, waiting for transfers between devices, local(): lax.psum(shares[0].astype(jnp.bfloat16), 'row').astype(jnp.float32)  50.5 us
    ppermute x3, waiting for transfers between devices, local(): lax.ppermute(ring[-1], 'rep', [(dev, (dev + 1) % 4) for dev in range(4)])  26.2 us
    ppermute x4, waiting for transfers between devices, from_behind(): return lax.ppermute(value, axis, pairs)  25.5 us
    reduce_scatter x1, waiting for transfers between devices, local(): lax.psum_scatter((own_part + from_next + from_prior).astype(jnp.bfloat16)...  25.2 us
    reduce_scatter x1, waiting for transfers between devices, local(): lax.psum_scatter(local_output.astype(jnp.bfloat16), 'rep', scatter_dimens...  22.4 us
    reduce_scatter x1, waiting for transfers between devices, local(): lax.psum_scatter(local_self.astype(jnp.bfloat16), 'rep', scatter_dimensio...  22.2 us
    scatter-add x1, other arithmetic, local(): spread.at[window_index.reshape(-1)]  9.53 us
    reduce_scatter x1, waiting for transfers between devices, local(): lax.psum_scatter(local_aggregate.astype(jnp.bfloat16), 'rep', scatter_dim...  5.55 us
  transfers between devices with their start and end apart: 13, of which 10 were waited for; matrix products, arithmetic and copies ran while one was open for 16% of the time, Pallas kernels for 0%

profile of v1, /device:TPU:0, one launch (start us, length us, event | category | flops | bytes accessed | tf_op | source)
XLA Modules:
  0.0 253.2 jit_solution(3386737388654672953)
XLA Ops:
  7.2 3.1 %collective-permute-start = (bf16[256,512]{1,0:T(8,128)(2,1)}, bf16[256,512]{1,0:T(8,128)(2,1)S(1)}, u32[]{:S(2)}, u32[]{:S(2)}) collective-permute-start(bf16[256,512]{1,0:T(8,128)(2,1)} %param.8), channel_id=1, source_target_pairs={{0,1},{1,2},{2,3},{3,0},{4,5},{5,6},{6,7},{7,4},{8,9},{9,10},{10,1... | collective-permute-start | bytes 786440 | tf_op jit(solution)/shard_map/ppermute | solution.py:37
  10.3 8.5 %collective-permute-done = bf16[256,512]{1,0:T(8,128)(2,1)S(1)} collective-permute-done((bf16[256,512]{1,0:T(8,128)(2,1)}, bf16[256,512]{1,0:T(8,128)(2,1)S(1)}, u32[]{:S(2)}, u32[]{:S(2)}) %collective-permute-start) | collective-permute-done | bytes 262176 | tf_op jit(solution)/shard_map/ppermute | solution.py:37
  18.9 9.3 %collective-permute-done.1 = bf16[256,512]{1,0:T(8,128)(2,1)S(1)} collective-permute-done((bf16[256,512]{1,0:T(8,128)(2,1)S(1)}, bf16[256,512]{1,0:T(8,128)(2,1)S(1)}, u32[]{:S(2)}, u32[]{:S(2)}) %collective-permute-start.1) | collective-permute-done | bytes 262176 | tf_op jit(solution)/shard_map/ppermute | solution.py:37
  28.2 8.4 %collective-permute-done.2 = bf16[256,512]{1,0:T(8,128)(2,1)S(1)} collective-permute-done((bf16[256,512]{1,0:T(8,128)(2,1)S(1)}, bf16[256,512]{1,0:T(8,128)(2,1)S(1)}, u32[]{:S(2)}, u32[]{:S(2)}) %collective-permute-start.2) | collective-permute-done | bytes 262176 | tf_op jit(solution)/shard_map/ppermute | solution.py:37
  38.5 22.4 %collective-permute-done.4 = bf16[1024,512]{1,0:T(8,128)(2,1)S(1)} collective-permute-done((bf16[1024,512]{1,0:T(8,128)(2,1)S(1)}, bf16[1024,512]{1,0:T(8,128)(2,1)S(1)}, u32[]{:S(2)}, u32[]{:S(2)}) %collective-permute-start.4) | collective-permute-done | bytes 1048608 | tf_op jit(solution)/shard_map/ppermute | solution.py:11
  60.9 3.1 %collective-permute-done.3 = bf16[1024,512]{1,0:T(8,128)(2,1)} collective-permute-done((bf16[1024,512]{1,0:T(8,128)(2,1)S(1)}, bf16[1024,512]{1,0:T(8,128)(2,1)}, u32[]{:S(2)}, u32[]{:S(2)}) %collective-permute-start.3) | collective-permute-done | bytes 1048608 | tf_op jit(solution)/shard_map/ppermute | solution.py:11
  64.0 2.8 %pad_maximum_fusion = bf16[3072,512]{1,0:T(8,128)(2,1)} fusion(bf16[1024,512]{1,0:T(8,128)(2,1)S(1)} %collective-permute-done.4, bf16[1024,512]{1,0:T(8,128)(2,1)S(1)} %constant_dynamic-slice_fusion, bf16[1024,512]{1,0:T(8,128)(2,1)} %collective-permute-done.3), kind=kLoop, calls=%fused_computation.2 | loop fusion | flops 9437184 | bytes 6291456 | tf_op jit(solution)/shard_map/concatenate | solution.py:43
  66.8 2.6 %gather_fusion = bf16[16,128,512]{2,1,0:T(8,128)(2,1)S(1)} fusion(bf16[24,128,512]{2,1,0:T(8,128)(2,1)} %bitcast.55, s32[1024]{0:T(1024)S(1)} %pad_clamp_fusion), kind=kCustom, calls=%fused_computation | custom fusion | bytes 4194368 | tf_op jit(solution)/shard_map/gather | solution.py:46
  77.2 2.7 %fusion.15 = f32[2,512,8,128]{3,1,2,0:T(8,128)} fusion(bf16[2,128,512,1]{2,1,3,0:T(8,128)(2,1)S(1)} %bitcast.59, bf16[2,8,128,128]{3,2,1,0:T(8,128)(2,1)S(1)} %copy-done), kind=kOutput, calls=%fused_computation.58 | convolution fusion | flops 268435456 | bytes 4980736 | tf_op jit(solution)/shard_map/bkji,bjf->bkif/dot_general | solution.py:66
  79.9 5.4 %copy.15 = f32[16,128,512]{2,1,0:T(8,128)} copy(f32[16,128,512]{1,2,0:T(8,128)} %bitcast.54) | data formatting | bytes 8388608 | tf_op jit(solution)/shard_map/reshape | solution.py:68
  85.3 3.5 %broadcast_in_dim.8 = f32[24,128,512]{2,1,0:T(8,128)} broadcast(f32[]{:T(128)} %constant.80.clone.1), dimensions={} | broadcast | bytes 6291460 | tf_op jit(solution)/shard_map/broadcast_in_dim | solution.py:67
  88.7 9.5 %scatter_fusion = f32[24,128,512]{2,1,0:T(8,128)} fusion(f32[24,128,512]{2,1,0:T(8,128)} %broadcast_in_dim.8, s32[16]{0:T(128)S(1)} %fusion.10, f32[16,128,512]{2,1,0:T(8,128)} %copy.15), kind=kCustom, calls=%fused_computation.1 | custom fusion | flops 1048576 | bytes 12582976 | tf_op jit(solution)/shard_map/scatter-add | solution.py:68
  98.3 3.3 %convert.4 = bf16[24,128,512]{2,1,0:T(8,128)(2,1)S(1)} convert(f32[24,128,512]{2,1,0:T(8,128)} %scatter_fusion) | non-fusion elementwise | flops 1572864 | bytes 9437184 | tf_op jit(solution)/shard_map/convert.1
  104.4 2.7 %collective-permute-start.5 = (bf16[1024,512]{1,0:T(8,128)(2,1)}, bf16[1024,512]{1,0:T(8,128)(2,1)}, u32[]{:S(2)}, u32[]{:S(2)}) collective-permute-start(bf16[1024,512]{1,0:T(8,128)(2,1)} %bitcast.12), channel_id=1, source_target_pairs={{0,28},{4,0},{8,4},{12,8},{16,12},{20,16},{24,20},{28,24},{1,29},{... | collective-permute-start | bytes 3145736 | tf_op jit(solution)/shard_map/ppermute | solution.py:11
  107.1 1.9 slice.22
  109.0 5.5 %reduce-scatter.12.cloned.1.call-done = bf16[128,512]{1,0:T(8,128)(2,1)} async-done(((bf16[512,512]{1,0:T(8,128)(2,1)}), bf16[128,512]{1,0:T(8,128)(2,1)}) %reduce-scatter.12.cloned.1.call-update) | async-done | bytes 131088 | tf_op jit(solution)/shard_map/reduce_scatter | solution.py:97
  114.6 22.4 %reduce-scatter.8.cloned.1.call-done = bf16[128,512]{1,0:T(8,128)(2,1)} async-done(((bf16[512,512]{1,0:T(8,128)(2,1)}), bf16[128,512]{1,0:T(8,128)(2,1)}) %reduce-scatter.8.cloned.1.call-update) | async-done | bytes 131088 | tf_op jit(solution)/shard_map/reduce_scatter | solution.py:91
  137.0 22.2 %reduce-scatter.14.cloned.1.call-done = bf16[128,512]{1,0:T(8,128)(2,1)} async-done(((bf16[512,512]{1,0:T(8,128)(2,1)}), bf16[128,512]{1,0:T(8,128)(2,1)}) %reduce-scatter.14.cloned.1.call-update) | async-done | bytes 131088 | tf_op jit(solution)/shard_map/reduce_scatter | solution.py:100
  159.3 3.2 %fusion.1 = bf16[1024,512]{1,0:T(8,128)(2,1)} fusion(f32[8,128,512]{2,1,0:T(8,128)S(1)} %slice.22, bf16[1024,512]{1,0:T(8,128)(2,1)} %collective-permute-done.6, bf16[1024,512]{1,0:T(8,128)(2,1)} %collective-permute-done.5), kind=kLoop, calls=%fused_computation.5 | loop fusion | flops 2621440 | bytes 5242880 | tf_op jit(solution)/shard_map/convert_element_type | solution.py:76
  162.6 2.3 fusion.4
  165.2 50.5 %all-reduce.3.cloned.1.call-done = (bf16[128,512]{1,0:T(8,128)(2,1)}, bf16[128,512]{1,0:T(8,128)(2,1)}, bf16[128,512]{1,0:T(8,128)(2,1)}, bf16[128,512]{1,0:T(8,128)(2,1)}) async-done(((bf16[128,512]{1,0:T(8,128)(2,1)}, bf16[128,512]{1,0:T(8,128)(2,1)}, bf16[128,512]{1,0:T(8,128)(2,1)}, bf16[128,512]{1,0:T(8,128)(2,1)}), (bf16[128,512]{1,0:T(8,128)(2,1)}, bf16[128,512]{1,0:T(8,128)(2,1)}, ...) | async-done | bytes 524304 | tf_op jit(solution)/shard_map/psum | solution.py:105
  215.8 1.8 convert_multiply_fusion.2
  217.6 1.8 convert_multiply_fusion
  219.4 25.2 %reduce-scatter.6.cloned.1.call-done = bf16[256,512]{1,0:T(8,128)(2,1)} async-done(((bf16[1024,512]{1,0:T(8,128)(2,1)}), bf16[256,512]{1,0:T(8,128)(2,1)}) %reduce-scatter.6.cloned.1.call-update) | async-done | bytes 262160 | tf_op jit(solution)/shard_map/reduce_scatter | solution.py:75
  (74 shorter events, 14.6 us)
Async XLA Ops:
  7.2 62.2 %copy-start = (bf16[2,8,128,128]{3,2,1,0:T(8,128)(2,1)S(1)}, bf16[2,8,128,128]{3,2,1,0:T(8,128)(2,1)}, u32[]{:S(2)}) copy-start(bf16[2,8,128,128]{3,2,1,0:T(8,128)(2,1)} %param.9) | copy-start | bytes 1572868
  7.2 30.5 %copy-start.1 = (bf16[256,512]{1,0:T(8,128)(2,1)S(1)}, bf16[256,512]{1,0:T(8,128)(2,1)}, u32[]{:S(2)}) copy-start(bf16[256,512]{1,0:T(8,128)(2,1)} %param.8) | copy-start | bytes 786436
  7.2 101.8 %reduce-scatter.10.cloned.1.call-start = ((), (), s32[]{:S(2)}) async-start(), calls=%async_computation.7 | async-start | bytes 655360 | tf_op jit(solution)/shard_map/reduce_scatter | solution.py:94
  7.2 11.6 %collective-permute-start = (bf16[256,512]{1,0:T(8,128)(2,1)}, bf16[256,512]{1,0:T(8,128)(2,1)S(1)}, u32[]{:S(2)}, u32[]{:S(2)}) collective-permute-start(bf16[256,512]{1,0:T(8,128)(2,1)} %param.8), channel_id=1, source_target_pairs={{0,1},{1,2},{2,3},{3,0},{4,5},{5,6},{6,7},{7,4},{8,9},{9,10},{10,1... | collective-permute-start | bytes 786440 | tf_op jit(solution)/shard_map/ppermute | solution.py:37
  18.9 9.3 %collective-permute-start.1 = (bf16[256,512]{1,0:T(8,128)(2,1)S(1)}, bf16[256,512]{1,0:T(8,128)(2,1)S(1)}, u32[]{:S(2)}, u32[]{:S(2)}) collective-permute-start(bf16[256,512]{1,0:T(8,128)(2,1)S(1)} %collective-permute-done), channel_id=1, source_target_pairs={{0,1},{1,2},{2,3},{3,0},{4,5},{5,6},{6,7},{7,4},{8,9},{9,10},{10,1... | collective-permute-start | bytes 786440 | tf_op jit(solution)/shard_map/ppermute | solution.py:37
  28.2 8.4 %collective-permute-start.2 = (bf16[256,512]{1,0:T(8,128)(2,1)S(1)}, bf16[256,512]{1,0:T(8,128)(2,1)S(1)}, u32[]{:S(2)}, u32[]{:S(2)}) collective-permute-start(bf16[256,512]{1,0:T(8,128)(2,1)S(1)} %collective-permute-done.1), channel_id=1, source_target_pairs={{0,1},{1,2},{2,3},{3,0},{4,5},{5,6},{6,7},{7,4},{8,9},{9,10},{10,1... | collective-permute-start | bytes 786440 | tf_op jit(solution)/shard_map/ppermute | solution.py:37
  37.8 23.1 %collective-permute-start.4 = (bf16[1024,512]{1,0:T(8,128)(2,1)S(1)}, bf16[1024,512]{1,0:T(8,128)(2,1)S(1)}, u32[]{:S(2)}, u32[]{:S(2)}) collective-permute-start(bf16[1024,512]{1,0:T(8,128)(2,1)S(1)} %constant_dynamic-slice_fusion), channel_id=1, source_target_pairs={{0,28},{4,0},{8,4},{12,8},{16,12},{20,16},{24,20},{28,24},{1,29},{... | collective-permute-start | bytes 3145736 | tf_op jit(solution)/shard_map/ppermute | solution.py:11
  37.9 26.1 %collective-permute-start.3 = (bf16[1024,512]{1,0:T(8,128)(2,1)S(1)}, bf16[1024,512]{1,0:T(8,128)(2,1)}, u32[]{:S(2)}, u32[]{:S(2)}) collective-permute-start(bf16[1024,512]{1,0:T(8,128)(2,1)S(1)} %constant_dynamic-slice_fusion), channel_id=1, source_target_pairs={{0,4},{4,8},{8,12},{12,16},{16,20},{20,24},{24,28},{28,0},{1,5},{5... | collective-permute-start | bytes 3145736 | tf_op jit(solution)/shard_map/ppermute | solution.py:11
  69.4 1.0 copy-start.4
  69.4 1.3 copy-start.2
  69.9 1.2 copy-start.9
  70.7 1.0 copy-start.6
  70.8 1.1 copy-start.10
  73.9 1.7 copy-start.12
  73.9 40.7 %reduce-scatter.12.cloned.1.call-start = ((), (), s32[]{:S(2)}) async-start(), calls=%async_computation.8 | async-start | bytes 655360 | tf_op jit(solution)/shard_map/reduce_scatter | solution.py:97
  75.5 1.4 copy-start.5
  75.5 61.5 %reduce-scatter.8.cloned.1.call-start = ((), (), s32[]{:S(2)}) async-start(), calls=%async_computation.6 | async-start | bytes 655360 | tf_op jit(solution)/shard_map/reduce_scatter | solution.py:91
  76.8 82.4 %reduce-scatter.14.cloned.1.call-start = ((), (), s32[]{:S(2)}) async-start(), calls=%async_computation.9 | async-start | bytes 655360 | tf_op jit(solution)/shard_map/reduce_scatter | solution.py:100
  103.2 56.2 %collective-permute-start.6 = (bf16[1024,512]{1,0:T(8,128)(2,1)}, bf16[1024,512]{1,0:T(8,128)(2,1)}, u32[]{:S(2)}, u32[]{:S(2)}) collective-permute-start(bf16[1024,512]{1,0:T(8,128)(2,1)} %bitcast.13), channel_id=1, source_target_pairs={{0,4},{4,8},{8,12},{12,16},{16,20},{20,24},{24,28},{28,0},{1,5},{5... | collective-permute-start | bytes 3145736 | tf_op jit(solution)/shard_map/ppermute | solution.py:11
  104.4 111.4 %all-reduce.3.cloned.1.call-start = ((), (), s32[]{:S(2)}) async-start(), calls=%async_computation.10 | async-start | bytes 1048576 | tf_op jit(solution)/shard_map/psum | solution.py:105
  104.4 54.9 %collective-permute-start.5 = (bf16[1024,512]{1,0:T(8,128)(2,1)}, bf16[1024,512]{1,0:T(8,128)(2,1)}, u32[]{:S(2)}, u32[]{:S(2)}) collective-permute-start(bf16[1024,512]{1,0:T(8,128)(2,1)} %bitcast.12), channel_id=1, source_target_pairs={{0,28},{4,0},{8,4},{12,8},{16,12},{20,16},{24,20},{28,24},{1,29},{... | collective-permute-start | bytes 3145736 | tf_op jit(solution)/shard_map/ppermute | solution.py:11
  159.3 85.3 %reduce-scatter.6.cloned.1.call-start = ((), (), s32[]{:S(2)}) async-start(), calls=%async_computation.5 | async-start | bytes 1310720 | tf_op jit(solution)/shard_map/reduce_scatter | solution.py:75
  162.6 2.3 copy-start.3
  162.6 2.3 copy-start.7
  (2 other events, 1.6 us)
Sparse Core Ops, SparseCore 0:
  74.0 18.1 reduce-scatter.9
  94.5 20.0 reduce-scatter.11
  116.9 20.0 reduce-scatter.7
  139.1 20.0 reduce-scatter.13
  162.4 53.3 all-reduce.2
  217.9 26.6 reduce-scatter.5
